TPU v7x, 32 devices: a whole 2x2x4 slice. The times are simulated.
32 devices in a mesh: src: 8 (over y, x, core), tgt: 4 (over z).
Axes of the slice: x: 2, y: 2, z: 4, core: 2. Of those that a mesh axis runs over, the one named last changes fastest.
Arguments:
- src_emb: bfloat16 [64, 131072], P(None, 'src'), may hold values from -3 to 3
- tgt_emb: bfloat16 [64, 65536], P(None, 'tgt'), may hold values from -3 to 3
- src_hidden: bfloat16 [64, 131072], P(None, 'src'), may hold values from -4 to 4
- growth: float32 [131072], P('src'), may hold values from -1 to 1
- tgt_mass: float32 [65536], P('tgt'), may hold values from 0.5 to 2
- pair_code: int32 [8, 4, 512], P('src', 'tgt'), may hold values from 0 to 16383, as said below
- pair_count: int32 [8, 4], P('src', 'tgt'), may hold values from 128 to 512, as said below
- block_batch: int32 [1024], P('src'), may hold values from 0 to 31
Outputs:
- src_potential: float32 [131072], P('src')
- tgt_potential: float32 [65536], P('tgt')
- tgt_grad: float32 [64, 65536], P(None, 'tgt')
- adapter_grad: float32 [32, 64, 64], P(('src', 'tgt'))
Inputs may be any that keep to these rules, and one draw needn't show every extreme that they name: `pair_code`: the codes of one device are distinct; among the first 128 entries of each device's list every one of its 128 source blocks and every one of its 128 target blocks appears. `pair_count`: in every draw some device has all 512 entries live.
All inputs are finite; a program needn't handle non-finite values.
Results may differ from a plain program's by a relative error of at most 0.0003.
Values sent between devices are 32-bit elements; how exact they have to be, the bound alone decides.
A program may use at most 192 MiB of HBM per device.

v0:
```python
import math
import jax
import jax.numpy as jnp
from jax import lax
from jax.sharding import PartitionSpec as P

BLK = 128
ENC_DEV = 1
ITERS = 2
entropy_scale = 0.5
update_power = 0.4
highest = lax.Precision.HIGHEST


def rescale(scaling, masses, totals):
    return jnp.sqrt(scaling) * jnp.power(masses / totals, update_power)


def pick_blocks(selector, blocks):
    picked = jnp.einsum(
        "gb,dbi->dgi", selector.astype(jnp.bfloat16), blocks, preferred_element_type=jnp.float32
    )
    return picked.astype(jnp.bfloat16)


def per_device(src_emb, tgt_emb, src_hidden, growth, tgt_mass, pair_code, pair_count, block_batch):
    feat_width = src_emb.shape[0]
    src_blocks = src_emb.shape[1] // BLK
    tgt_blocks = tgt_emb.shape[1] // BLK
    src_cells = src_blocks * BLK
    tgt_cells = tgt_blocks * BLK
    slot_count = pair_code.shape[2]
    group_size = math.gcd(slot_count, 64)
    group_count = slot_count // group_size
    pair_slots = pair_code.reshape(slot_count)
    alive_mask = (jnp.arange(slot_count, dtype=jnp.int32) < pair_count.reshape(())).astype(
        jnp.float32
    )
    src_ids = pair_slots // tgt_blocks
    tgt_ids = pair_slots % tgt_blocks
    src_select = (src_ids[:, None] == jnp.arange(src_blocks, dtype=jnp.int32)[None, :]).astype(
        jnp.float32
    )
    tgt_select = (tgt_ids[:, None] == jnp.arange(tgt_blocks, dtype=jnp.int32)[None, :]).astype(
        jnp.float32
    )
    x_blocks = src_emb.reshape(feat_width, src_blocks, BLK)
    y_blocks = tgt_emb.reshape(feat_width, tgt_blocks, BLK)
    x_norms = jnp.sum(jnp.square(x_blocks.astype(jnp.float32)), axis=0)
    y_norms = jnp.sum(jnp.square(y_blocks.astype(jnp.float32)), axis=0)
    src_sel_groups = src_select.reshape(group_count, group_size, src_blocks)
    tgt_sel_groups = tgt_select.reshape(group_count, group_size, tgt_blocks)

    def kernel_group(inputs):
        src_sel, tgt_sel, alive_group = inputs
        x_part = pick_blocks(src_sel, x_blocks)
        y_part = pick_blocks(tgt_sel, y_blocks)
        inner_prods = jnp.einsum("dgi,dgj->gij", x_part, y_part, preferred_element_type=jnp.float32)
        x_sq = jnp.dot(src_sel, x_norms, precision=highest)
        y_sq = jnp.dot(tgt_sel, y_norms, precision=highest)
        distance = (x_sq[:, :, None] + y_sq[:, None, :] - 2.0 * inner_prods) / feat_width
        return jnp.exp(-distance / entropy_scale) * alive_group[:, None, None]

    kernel = lax.map(
        kernel_group, (src_sel_groups, tgt_sel_groups, alive_mask.reshape(group_count, group_size))
    )
    kernel = kernel.reshape(slot_count, BLK, BLK)
    src_mass = jnp.exp(growth)
    src_scale = jnp.ones((src_cells,), jnp.float32)
    tgt_scale = jnp.ones((tgt_cells,), jnp.float32)
    for iteration in range(ITERS):
        tgt_picked = jnp.dot(tgt_select, tgt_scale.reshape(tgt_blocks, BLK), precision=highest)
        src_picked = jnp.dot(src_select, src_scale.reshape(src_blocks, BLK), precision=highest)
        row_slots = jnp.einsum("pij,pj->pi", kernel, tgt_picked, precision=highest)
        col_slots = jnp.einsum("pij,pi->pj", kernel, src_picked, precision=highest)
        row_part = jnp.dot(src_select.T, row_slots, precision=highest).reshape(src_cells)
        col_part = jnp.dot(tgt_select.T, col_slots, precision=highest).reshape(tgt_cells)
        row_sums = lax.psum(row_part, "tgt")
        col_sums = lax.psum(col_part, "src")
        src_scale, tgt_scale = (
            rescale(src_scale, src_mass, row_sums),
            rescale(tgt_scale, tgt_mass, col_sums),
        )
    src_potential = entropy_scale * jnp.log(src_scale)
    tgt_potential = entropy_scale * jnp.log(tgt_scale)
    src_blocked = src_scale.reshape(src_blocks, BLK)
    tgt_blocked = tgt_scale.reshape(tgt_blocks, BLK)

    def gradient_group(carry, inputs):
        dx_total, dy_total = carry
        src_sel, tgt_sel, kernel_part = inputs
        row_scale = jnp.dot(src_sel, src_blocked, precision=highest)
        col_scale = jnp.dot(tgt_sel, tgt_blocked, precision=highest)
        transport = row_scale[:, :, None] * kernel_part * col_scale[:, None, :]
        plan_bf16 = transport.astype(jnp.bfloat16)
        x_part = pick_blocks(src_sel, x_blocks)
        y_part = pick_blocks(tgt_sel, y_blocks)
        pulled = jnp.einsum("gij,dgj->dgi", plan_bf16, y_part, preferred_element_type=jnp.float32)
        pushed = jnp.einsum("gij,dgi->dgj", plan_bf16, x_part, preferred_element_type=jnp.float32)
        dx_term = jnp.sum(transport, axis=2)[None] * x_part.astype(jnp.float32) - pulled
        dy_term = jnp.sum(transport, axis=1)[None] * y_part.astype(jnp.float32) - pushed
        dx_total = dx_total + jnp.einsum("gb,dgi->dbi", src_sel, dx_term, precision=highest)
        dy_total = dy_total + jnp.einsum("gb,dgi->dbi", tgt_sel, dy_term, precision=highest)
        return ((dx_total, dy_total), None)

    start_grads = (
        jnp.zeros((feat_width, src_blocks, BLK), jnp.float32),
        jnp.zeros((feat_width, tgt_blocks, BLK), jnp.float32),
    )
    (dx_total, dy_total), _ = lax.scan(
        gradient_group,
        start_grads,
        (src_sel_groups, tgt_sel_groups, kernel.reshape(group_count, group_size, BLK, BLK)),
    )
    tgt_grad = lax.psum(dy_total.reshape(feat_width, tgt_cells), "src")
    hidden_blocks = src_hidden.reshape(feat_width, src_blocks, BLK)
    grad_share = lax.psum_scatter(dx_total, "tgt", scatter_dimension=1, tiled=True)
    share_blocks = grad_share.shape[1]
    first_block = lax.axis_index("tgt") * share_blocks
    hidden_share = lax.dynamic_slice_in_dim(hidden_blocks, first_block, share_blocks, 1)
    batch_share = lax.dynamic_slice_in_dim(block_batch, first_block, share_blocks, 0)
    outer = (
        jnp.einsum("dbi,ebi->bde", hidden_share.astype(jnp.float32), grad_share, precision=highest)
        / BLK
    )
    wanted = jnp.arange(ENC_DEV * lax.axis_size(("src", "tgt")), dtype=jnp.int32)
    owners = (batch_share[None, :] == wanted[:, None]).astype(jnp.float32)
    adapter_grad = lax.psum_scatter(
        jnp.einsum("kb,bde->kde", owners, outer, precision=highest),
        ("src", "tgt"),
        scatter_dimension=0,
        tiled=True,
    )
    return (src_potential, tgt_potential, tgt_grad, adapter_grad)


def solution(mesh):
    in_specs = (
        P(None, "src"),
        P(None, "tgt"),
        P(None, "src"),
        P("src"),
        P("tgt"),
        P("src", "tgt", None),
        P("src", "tgt"),
        P("src"),
    )
    out_specs = (P("src"), P("tgt"), P(None, "tgt"), P(("src", "tgt"), None, None))
    return jax.shard_map(
        per_device, mesh=mesh, in_specs=in_specs, out_specs=out_specs, check_vma=False
    )
```

profile of v0, /device:TPU:0, one launch (start us, length us, event | category | flops | bytes accessed | tf_op | source)
XLA Modules:
  0.0 1027.3 jit_solution(16935787503366914984)
XLA Ops:
  17.6 84.6 %while.23 = (s32[]{:T(128)}, f32[8,64,128,128]{3,2,1,0:T(8,128)}, f32[8,64,128]{2,1,0:T(8,128)S(1)}, f32[128,128]{1,0:T(8,128)S(1)}, f32[8,64,128]{2,1,0:T(8,128...) while((s32[]{:T(128)}, f32[8,64,128,128]{3,2,1,0:T(8,128)}, ...), condition=%wide.region_3.4_spmd, body=%wide.region_2.3_spmd.sunk | while | flops 435159040 | bytes 21334412 | solution.py:64
  21.5 6.6 bitcast_dynamic-update-slice_fusion.2
  32.1 6.6 bitcast_dynamic-update-slice_fusion.2
  42.7 6.6 bitcast_dynamic-update-slice_fusion.2
  53.3 6.6 bitcast_dynamic-update-slice_fusion.2
  63.8 6.6 bitcast_dynamic-update-slice_fusion.2
  74.4 6.6 bitcast_dynamic-update-slice_fusion.2
  85.0 6.6 bitcast_dynamic-update-slice_fusion.2
  95.5 6.6 bitcast_dynamic-update-slice_fusion.2
  102.5 55.7 %fusion.97 = f32[512,1,128]{2,1,0:T(1,128)S(1)} fusion(f32[512,128,128]{2,1,0:T(8,128)} %bitcast.228, f32[512,128,1]{1,2,0:T(1,128)S(1)} %bitcast.246), kind=kOutput, calls=%fused_computation.137 | convolution fusion | flops 100663296 | bytes 34078720 | tf_op jit(solution)/shard_map/pij,pj->pi/dot_general | solution.py:74
  160.0 32.0 %fusion.98 = f32[512,1,128]{2,1,0:T(1,128)S(1)} fusion(f32[512,128,128]{2,1,0:T(8,128)} %bitcast.229, f32[512,128,1]{1,2,0:T(1,128)S(1)} %bitcast.248), kind=kOutput, calls=%fused_computation.138 | convolution fusion | flops 100663296 | bytes 34078720 | tf_op jit(solution)/shard_map/pij,pi->pj/dot_general | solution.py:75
  197.7 32.3 %fusion.100 = f32[512,1,128]{2,1,0:T(1,128)S(1)} fusion(f32[512,128,128]{2,1,0:T(8,128)} %bitcast.230, f32[512,128,1]{1,2,0:T(1,128)S(1)} %bitcast.249), kind=kOutput, calls=%fused_computation.140 | convolution fusion | flops 100663296 | bytes 34078720 | tf_op jit(solution)/shard_map/pij,pi->pj/dot_general | solution.py:75
  231.3 53.3 %all-reduce.12.cloned.1.call-done = (f32[16384]{0:T(1024)}, f32[16384]{0:T(1024)}) async-done(((f32[16384]{0:T(1024)}, f32[16384]{0:T(1024)}), (f32[16384]{0:T(1024)}, f32[16384]{0:T(1024)})) %all-reduce.12.cloned.1.call-update) | async-done | bytes 131088 | tf_op jit(solution)/shard_map/psum | solution.py:79
  285.8 55.9 %fusion.99 = f32[512,1,128]{2,1,0:T(1,128)S(1)} fusion(f32[512,128,128]{2,1,0:T(8,128)} %bitcast.231, f32[512,128,1]{1,2,0:T(1,128)S(1)} %bitcast.247), kind=kOutput, calls=%fused_computation.139 | convolution fusion | flops 100663296 | bytes 34078720 | tf_op jit(solution)/shard_map/pij,pj->pi/dot_general | solution.py:74
  343.7 33.0 %all-reduce.8.cloned.1.call-done = f32[16384]{0:T(1024)} async-done(((f32[16384]{0:T(1024)}), f32[16384]{0:T(1024)}) %all-reduce.8.cloned.1.call-update) | async-done | bytes 65552 | tf_op jit(solution)/shard_map/psum | solution.py:78
  378.3 330.9 %while.24 = (s32[]{:T(128)}, f32[64,128,128]{1,2,0:T(8,128)}, f32[64,128,128]{1,2,0:T(8,128)}, f32[8,64,128]{2,1,0:T(8,128)S(1)}, f32[128,128]{1,0:T(8,128)}, /*...) while((s32[]{:T(128)}, f32[64,128,128]{1,2,0:T(8,128)}, ...), condition=%wide.region_11.12_spmd.clone, body=%wide.region_8.11_spmd.clone.sunk | while | flops 2191507456 | bytes 61508292 | solution.py:110
  381.0 5.4 fusion.193
  392.9 10.6 %bitcast_add_fusion.5 = f32[64,128,128]{1,2,0:T(8,128)} fusion(f32[64,128,128]{1,2,0:T(8,128)} %get-tuple-element.360, f32[64,64,128]{2,1,0:T(8,128)} %fusion.193, bf16[64,64,128]{2,1,0:T(8,128)(2,1)} %fusion.187, pred[]{:T(512)S(6)} %compare.16, f32[64,128]{1,0:T(8,128)S(1)} %get-tuple-element.315, f32[8,64,128]{2,1,0:T(8,128)} %get-tuple-element.376, ...), kind=kOutput, calls=%fused_computation.23.clone.1 | convolution fusion | flops 808976384 | bytes 11600385 | tf_op jit(solution)/shard_map/while/body/eval_jaxpr/gb,dgi->dbi/dot_general | solution.py:103
  408.2 9.7 bitcast_add_fusion.4
  420.5 5.4 fusion.193
  432.3 11.2 %bitcast_add_fusion.5 = f32[64,128,128]{1,2,0:T(8,128)} fusion(f32[64,128,128]{1,2,0:T(8,128)} %get-tuple-element.360, f32[64,64,128]{2,1,0:T(8,128)} %fusion.193, bf16[64,64,128]{2,1,0:T(8,128)(2,1)} %fusion.187, pred[]{:T(512)S(6)} %compare.16, f32[64,128]{1,0:T(8,128)S(1)} %get-tuple-element.315, f32[8,64,128]{2,1,0:T(8,128)} %get-tuple-element.376, ...), kind=kOutput, calls=%fused_computation.23.clone.1 | convolution fusion | flops 808976384 | bytes 11600385 | tf_op jit(solution)/shard_map/while/body/eval_jaxpr/gb,dgi->dbi/dot_general | solution.py:103
  443.5 4.7 fusion.190
  448.2 11.3 %bitcast_add_fusion.4 = f32[64,128,128]{1,2,0:T(8,128)} fusion(f32[64,128,128]{1,2,0:T(8,128)} %get-tuple-element.359, f32[64,64,128]{2,1,0:T(8,128)S(1)} %fusion.190, bf16[64,64,128]{2,1,0:T(8,128)(2,1)S(1)} %fusion.191, pred[]{:T(512)S(6)} %compare.16, f32[64,128]{1,0:T(8,128)S(1)} %get-tuple-element.314, ...), kind=kOutput, calls=%fused_computation.24.clone.1 | convolution fusion | flops 808976384 | bytes 11599877 | tf_op jit(solution)/shard_map/while/body/eval_jaxpr/gb,dgi->dbi/dot_general | solution.py:102
  462.0 5.4 fusion.193
  473.9 11.2 %bitcast_add_fusion.5 = f32[64,128,128]{1,2,0:T(8,128)} fusion(f32[64,128,128]{1,2,0:T(8,128)} %get-tuple-element.360, f32[64,64,128]{2,1,0:T(8,128)} %fusion.193, bf16[64,64,128]{2,1,0:T(8,128)(2,1)} %fusion.187, pred[]{:T(512)S(6)} %compare.16, f32[64,128]{1,0:T(8,128)S(1)} %get-tuple-element.315, f32[8,64,128]{2,1,0:T(8,128)} %get-tuple-element.376, ...), kind=kOutput, calls=%fused_computation.23.clone.1 | convolution fusion | flops 808976384 | bytes 11600385 | tf_op jit(solution)/shard_map/while/body/eval_jaxpr/gb,dgi->dbi/dot_general | solution.py:103
  489.8 11.3 %bitcast_add_fusion.4 = f32[64,128,128]{1,2,0:T(8,128)} fusion(f32[64,128,128]{1,2,0:T(8,128)} %get-tuple-element.359, f32[64,64,128]{2,1,0:T(8,128)S(1)} %fusion.190, bf16[64,64,128]{2,1,0:T(8,128)(2,1)S(1)} %fusion.191, pred[]{:T(512)S(6)} %compare.16, f32[64,128]{1,0:T(8,128)S(1)} %get-tuple-element.314, ...), kind=kOutput, calls=%fused_computation.24.clone.1 | convolution fusion | flops 808976384 | bytes 11599877 | tf_op jit(solution)/shard_map/while/body/eval_jaxpr/gb,dgi->dbi/dot_general | solution.py:102
  503.6 5.4 fusion.193
  515.5 11.2 %bitcast_add_fusion.5 = f32[64,128,128]{1,2,0:T(8,128)} fusion(f32[64,128,128]{1,2,0:T(8,128)} %get-tuple-element.360, f32[64,64,128]{2,1,0:T(8,128)} %fusion.193, bf16[64,64,128]{2,1,0:T(8,128)(2,1)} %fusion.187, pred[]{:T(512)S(6)} %compare.16, f32[64,128]{1,0:T(8,128)S(1)} %get-tuple-element.315, f32[8,64,128]{2,1,0:T(8,128)} %get-tuple-element.376, ...), kind=kOutput, calls=%fused_computation.23.clone.1 | convolution fusion | flops 808976384 | bytes 11600385 | tf_op jit(solution)/shard_map/while/body/eval_jaxpr/gb,dgi->dbi/dot_general | solution.py:103
  526.7 4.7 fusion.190
  531.4 11.3 %bitcast_add_fusion.4 = f32[64,128,128]{1,2,0:T(8,128)} fusion(f32[64,128,128]{1,2,0:T(8,128)} %get-tuple-element.359, f32[64,64,128]{2,1,0:T(8,128)S(1)} %fusion.190, bf16[64,64,128]{2,1,0:T(8,128)(2,1)S(1)} %fusion.191, pred[]{:T(512)S(6)} %compare.16, f32[64,128]{1,0:T(8,128)S(1)} %get-tuple-element.314, ...), kind=kOutput, calls=%fused_computation.24.clone.1 | convolution fusion | flops 808976384 | bytes 11599877 | tf_op jit(solution)/shard_map/while/body/eval_jaxpr/gb,dgi->dbi/dot_general | solution.py:102
  545.2 5.4 fusion.193
  557.0 11.2 %bitcast_add_fusion.5 = f32[64,128,128]{1,2,0:T(8,128)} fusion(f32[64,128,128]{1,2,0:T(8,128)} %get-tuple-element.360, f32[64,64,128]{2,1,0:T(8,128)} %fusion.193, bf16[64,64,128]{2,1,0:T(8,128)(2,1)} %fusion.187, pred[]{:T(512)S(6)} %compare.16, f32[64,128]{1,0:T(8,128)S(1)} %get-tuple-element.315, f32[8,64,128]{2,1,0:T(8,128)} %get-tuple-element.376, ...), kind=kOutput, calls=%fused_computation.23.clone.1 | convolution fusion | flops 808976384 | bytes 11600385 | tf_op jit(solution)/shard_map/while/body/eval_jaxpr/gb,dgi->dbi/dot_general | solution.py:103
  572.9 11.3 %bitcast_add_fusion.4 = f32[64,128,128]{1,2,0:T(8,128)} fusion(f32[64,128,128]{1,2,0:T(8,128)} %get-tuple-element.359, f32[64,64,128]{2,1,0:T(8,128)S(1)} %fusion.190, bf16[64,64,128]{2,1,0:T(8,128)(2,1)S(1)} %fusion.191, pred[]{:T(512)S(6)} %compare.16, f32[64,128]{1,0:T(8,128)S(1)} %get-tuple-element.314, ...), kind=kOutput, calls=%fused_computation.24.clone.1 | convolution fusion | flops 808976384 | bytes 11599877 | tf_op jit(solution)/shard_map/while/body/eval_jaxpr/gb,dgi->dbi/dot_general | solution.py:102
  586.7 5.4 fusion.193
  598.6 11.2 %bitcast_add_fusion.5 = f32[64,128,128]{1,2,0:T(8,128)} fusion(f32[64,128,128]{1,2,0:T(8,128)} %get-tuple-element.360, f32[64,64,128]{2,1,0:T(8,128)} %fusion.193, bf16[64,64,128]{2,1,0:T(8,128)(2,1)} %fusion.187, pred[]{:T(512)S(6)} %compare.16, f32[64,128]{1,0:T(8,128)S(1)} %get-tuple-element.315, f32[8,64,128]{2,1,0:T(8,128)} %get-tuple-element.376, ...), kind=kOutput, calls=%fused_computation.23.clone.1 | convolution fusion | flops 808976384 | bytes 11600385 | tf_op jit(solution)/shard_map/while/body/eval_jaxpr/gb,dgi->dbi/dot_general | solution.py:103
  614.5 11.3 %bitcast_add_fusion.4 = f32[64,128,128]{1,2,0:T(8,128)} fusion(f32[64,128,128]{1,2,0:T(8,128)} %get-tuple-element.359, f32[64,64,128]{2,1,0:T(8,128)S(1)} %fusion.190, bf16[64,64,128]{2,1,0:T(8,128)(2,1)S(1)} %fusion.191, pred[]{:T(512)S(6)} %compare.16, f32[64,128]{1,0:T(8,128)S(1)} %get-tuple-element.314, ...), kind=kOutput, calls=%fused_computation.24.clone.1 | convolution fusion | flops 808976384 | bytes 11599877 | tf_op jit(solution)/shard_map/while/body/eval_jaxpr/gb,dgi->dbi/dot_general | solution.py:102
  628.3 5.4 fusion.193
  640.2 11.2 %bitcast_add_fusion.5 = f32[64,128,128]{1,2,0:T(8,128)} fusion(f32[64,128,128]{1,2,0:T(8,128)} %get-tuple-element.360, f32[64,64,128]{2,1,0:T(8,128)} %fusion.193, bf16[64,64,128]{2,1,0:T(8,128)(2,1)} %fusion.187, pred[]{:T(512)S(6)} %compare.16, f32[64,128]{1,0:T(8,128)S(1)} %get-tuple-element.315, f32[8,64,128]{2,1,0:T(8,128)} %get-tuple-element.376, ...), kind=kOutput, calls=%fused_computation.23.clone.1 | convolution fusion | flops 808976384 | bytes 11600385 | tf_op jit(solution)/shard_map/while/body/eval_jaxpr/gb,dgi->dbi/dot_general | solution.py:103
  656.1 11.3 %bitcast_add_fusion.4 = f32[64,128,128]{1,2,0:T(8,128)} fusion(f32[64,128,128]{1,2,0:T(8,128)} %get-tuple-element.359, f32[64,64,128]{2,1,0:T(8,128)S(1)} %fusion.190, bf16[64,64,128]{2,1,0:T(8,128)(2,1)S(1)} %fusion.191, pred[]{:T(512)S(6)} %compare.16, f32[64,128]{1,0:T(8,128)S(1)} %get-tuple-element.314, ...), kind=kOutput, calls=%fused_computation.24.clone.1 | convolution fusion | flops 808976384 | bytes 11599877 | tf_op jit(solution)/shard_map/while/body/eval_jaxpr/gb,dgi->dbi/dot_general | solution.py:102
  669.9 5.4 fusion.193
  681.7 11.2 %bitcast_add_fusion.5 = f32[64,128,128]{1,2,0:T(8,128)} fusion(f32[64,128,128]{1,2,0:T(8,128)} %get-tuple-element.360, f32[64,64,128]{2,1,0:T(8,128)} %fusion.193, bf16[64,64,128]{2,1,0:T(8,128)(2,1)} %fusion.187, pred[]{:T(512)S(6)} %compare.16, f32[64,128]{1,0:T(8,128)S(1)} %get-tuple-element.315, f32[8,64,128]{2,1,0:T(8,128)} %get-tuple-element.376, ...), kind=kOutput, calls=%fused_computation.23.clone.1 | convolution fusion | flops 808976384 | bytes 11600385 | tf_op jit(solution)/shard_map/while/body/eval_jaxpr/gb,dgi->dbi/dot_general | solution.py:103
  697.7 11.3 %bitcast_add_fusion.4 = f32[64,128,128]{1,2,0:T(8,128)} fusion(f32[64,128,128]{1,2,0:T(8,128)} %get-tuple-element.359, f32[64,64,128]{2,1,0:T(8,128)S(1)} %fusion.190, bf16[64,64,128]{2,1,0:T(8,128)(2,1)S(1)} %fusion.191, pred[]{:T(512)S(6)} %compare.16, f32[64,128]{1,0:T(8,128)S(1)} %get-tuple-element.314, ...), kind=kOutput, calls=%fused_computation.24.clone.1 | convolution fusion | flops 808976384 | bytes 11599877 | tf_op jit(solution)/shard_map/while/body/eval_jaxpr/gb,dgi->dbi/dot_general | solution.py:102
  709.1 5.4 copy.15
  714.6 5.6 copy.14
  720.2 6.9 copy.62
  729.5 61.7 %reduce-scatter.3.cloned.1.call-done = f32[64,32,128]{2,0,1:T(8,128)} async-done(((f32[64,128,128]{2,0,1:T(8,128)}), f32[64,32,128]{2,0,1:T(8,128)}) %reduce-scatter.3.cloned.1.call-update) | async-done | bytes 1048592 | tf_op jit(solution)/shard_map/reduce_scatter | solution.py:117
  796.3 79.4 %all-reduce.10.cloned.1.call-done = f32[64,16384]{1,0:T(8,128)} async-done(((f32[64,16384]{1,0:T(8,128)}), f32[64,16384]{1,0:T(8,128)}) %all-reduce.10.cloned.1.call-update) | async-done | bytes 4194320 | tf_op jit(solution)/shard_map/psum | solution.py:115
  875.7 139.8 %reduce-scatter.5.cloned.1.call-done = f32[1,64,64]{2,1,0:T(8,128)} async-done(((f32[32,64,64]{2,1,0:T(8,128)}), f32[1,64,64]{2,1,0:T(8,128)}) %reduce-scatter.5.cloned.1.call-update) | async-done | bytes 16400 | tf_op jit(solution)/shard_map/reduce_scatter | solution.py:128
  (194 shorter events, 166.4 us)
Async XLA Ops:
  7.2 189.4 %all-reduce.6.cloned.1.call-start = ((), (), s32[]{:S(2)}) async-start(), calls=%async_computation.2 | async-start | bytes 131072 | tf_op jit(solution)/shard_map/psum | solution.py:78
  9.2 4.4 copy-start.3
  17.6 84.6 %copy-start.9 = (s32[1,1,512]{2,1,0:T(1,128)S(1)}, s32[1,1,512]{2,1,0:T(1,128)}, u32[]{:S(2)}) copy-start(s32[1,1,512]{2,1,0:T(1,128)} %param.17) | copy-start | bytes 6148
  17.6 1.6 copy-start
  28.1 1.6 copy-start
  38.7 1.6 copy-start
  49.3 1.6 copy-start
  59.9 1.6 copy-start
  70.4 1.6 copy-start
  81.0 1.6 copy-start
  91.6 1.6 copy-start
  159.4 125.2 %all-reduce.12.cloned.1.call-start = ((), (), s32[]{:S(2)}) async-start(), calls=%async_computation.7 | async-start | bytes 262144 | tf_op jit(solution)/shard_map/psum | solution.py:79
  160.0 36.6 %copy-start.5 = (f32[16384]{0:T(1024)S(1)}, f32[16384]{0:T(1024)}, u32[]{:S(2)}) copy-start(f32[16384]{0:T(1024)} %param.15) | copy-start | bytes 196612
  197.7 86.9 %copy-start.4 = (f32[16384]{0:T(1024)S(1)}, f32[16384]{0:T(1024)}, u32[]{:S(2)}) copy-start(f32[16384]{0:T(1024)} %param.16) | copy-start | bytes 196612
  231.2 145.4 %all-reduce.8.cloned.1.call-start = ((), (), s32[]{:S(2)}) async-start(), calls=%async_computation.3 | async-start | bytes 131072 | tf_op jit(solution)/shard_map/psum | solution.py:78
  285.8 57.1 %copy-start.7 = (f32[16384]{0:T(1024)S(1)}, f32[16384]{0:T(1024)}, u32[]{:S(2)}) copy-start(f32[16384]{0:T(1024)} %get-tuple-element.184) | copy-start | bytes 196612
  285.8 57.1 %copy-start.8 = (f32[16384]{0:T(1024)S(1)}, f32[16384]{0:T(1024)}, u32[]{:S(2)}) copy-start(f32[16384]{0:T(1024)} %get-tuple-element.185) | copy-start | bytes 196612
  285.8 90.9 %copy-start.6 = (f32[16384]{0:T(1024)S(1)}, f32[16384]{0:T(1024)}, u32[]{:S(2)}) copy-start(f32[16384]{0:T(1024)} %all-reduce.6.cloned.1.call-done) | copy-start | bytes 196612
  342.8 448.4 %reduce-scatter.3.cloned.1.call-start = ((), (), s32[]{:S(2)}) async-start(), calls=%async_computation.5 | async-start | bytes 5242880 | tf_op jit(solution)/shard_map/reduce_scatter | solution.py:117
  381.0 9.7 copy-start.1
  392.9 10.6 %copy-start.2 = (bf16[64,64,128]{2,1,0:T(8,128)(2,1)S(1)}, bf16[64,64,128]{2,1,0:T(8,128)(2,1)}, u32[]{:S(2)}) copy-start(bf16[64,64,128]{2,1,0:T(8,128)(2,1)} %fusion.187) | copy-start | bytes 3145732 | tf_op jit(solution)/shard_map/while
  420.4 9.7 copy-start.1
  432.3 11.2 %copy-start.2 = (bf16[64,64,128]{2,1,0:T(8,128)(2,1)S(1)}, bf16[64,64,128]{2,1,0:T(8,128)(2,1)}, u32[]{:S(2)}) copy-start(bf16[64,64,128]{2,1,0:T(8,128)(2,1)} %fusion.187) | copy-start | bytes 3145732 | tf_op jit(solution)/shard_map/while
  462.0 9.7 copy-start.1
  473.9 11.2 %copy-start.2 = (bf16[64,64,128]{2,1,0:T(8,128)(2,1)S(1)}, bf16[64,64,128]{2,1,0:T(8,128)(2,1)}, u32[]{:S(2)}) copy-start(bf16[64,64,128]{2,1,0:T(8,128)(2,1)} %fusion.187) | copy-start | bytes 3145732 | tf_op jit(solution)/shard_map/while
  503.6 9.7 copy-start.1
  515.5 11.2 %copy-start.2 = (bf16[64,64,128]{2,1,0:T(8,128)(2,1)S(1)}, bf16[64,64,128]{2,1,0:T(8,128)(2,1)}, u32[]{:S(2)}) copy-start(bf16[64,64,128]{2,1,0:T(8,128)(2,1)} %fusion.187) | copy-start | bytes 3145732 | tf_op jit(solution)/shard_map/while
  545.2 9.7 copy-start.1
  557.0 11.2 %copy-start.2 = (bf16[64,64,128]{2,1,0:T(8,128)(2,1)S(1)}, bf16[64,64,128]{2,1,0:T(8,128)(2,1)}, u32[]{:S(2)}) copy-start(bf16[64,64,128]{2,1,0:T(8,128)(2,1)} %fusion.187) | copy-start | bytes 3145732 | tf_op jit(solution)/shard_map/while
  586.7 9.7 copy-start.1
  598.6 11.2 %copy-start.2 = (bf16[64,64,128]{2,1,0:T(8,128)(2,1)S(1)}, bf16[64,64,128]{2,1,0:T(8,128)(2,1)}, u32[]{:S(2)}) copy-start(bf16[64,64,128]{2,1,0:T(8,128)(2,1)} %fusion.187) | copy-start | bytes 3145732 | tf_op jit(solution)/shard_map/while
  628.3 9.7 copy-start.1
  640.2 11.2 %copy-start.2 = (bf16[64,64,128]{2,1,0:T(8,128)(2,1)S(1)}, bf16[64,64,128]{2,1,0:T(8,128)(2,1)}, u32[]{:S(2)}) copy-start(bf16[64,64,128]{2,1,0:T(8,128)(2,1)} %fusion.187) | copy-start | bytes 3145732 | tf_op jit(solution)/shard_map/while
  669.9 9.7 copy-start.1
  681.7 11.2 %copy-start.2 = (bf16[64,64,128]{2,1,0:T(8,128)(2,1)S(1)}, bf16[64,64,128]{2,1,0:T(8,128)(2,1)}, u32[]{:S(2)}) copy-start(bf16[64,64,128]{2,1,0:T(8,128)(2,1)} %fusion.187) | copy-start | bytes 3145732 | tf_op jit(solution)/shard_map/while
  714.6 161.1 %all-reduce.10.cloned.1.call-start = ((), (), s32[]{:S(2)}) async-start(), calls=%async_computation.4 | async-start | bytes 8388608 | tf_op jit(solution)/shard_map/psum | solution.py:115
  727.1 2.3 copy-start.10
  727.2 288.3 %reduce-scatter.5.cloned.1.call-start = ((), (), s32[]{:S(2)}) async-start(), calls=%async_computation.6 | async-start | bytes 1081344 | tf_op jit(solution)/shard_map/reduce_scatter | solution.py:128
Sparse Core Ops, SparseCore 0:
  159.5 36.9 all-reduce.5
  231.4 53.2 all-reduce.11
  343.0 33.6 all-reduce.7
  714.7 76.4 reduce-scatter.2
  794.3 81.3 all-reduce.9
  878.4 137.0 reduce-scatter.4
where the time goes:
time: 1040 us; the launch traced here: 1030 us
  matrix products  558 us (54%)
  waiting for transfers between devices  371 us (36%)
  other arithmetic  41.4 us (4%)
  local copies, waits for them, and re-layouts  40.3 us (4%)
  between operations  15.4 us (1%)
    reduce_scatter x1, waiting for transfers between devices, per_device(): lax.psum_scatter(jnp.einsum('kb,bde->kde', owners, outer, precision=highe...  140 us
    dot_general x2, matrix products, per_device(): row_slots = jnp.einsum('pij,pj->pi', kernel, tgt_picked, precision=highest)  112 us
    dot_general x8, matrix products, gradient_group(): jnp.einsum('gb,dgi->dbi', tgt_sel, dy_term, precision=highest)  89 us
    dot_general x8, matrix products, gradient_group(): jnp.einsum('gb,dgi->dbi', src_sel, dx_term, precision=highest)  88.5 us
    psum x1, waiting for transfers between devices, per_device(): tgt_grad = lax.psum(dy_total.reshape(feat_width, tgt_cells), 'src')  79.4 us
    dot_general x2, matrix products, per_device(): col_slots = jnp.einsum('pij,pi->pj', kernel, src_picked, precision=highest)  64.3 us
    reduce_scatter x1, waiting for transfers between devices, per_device(): lax.psum_scatter(dx_total, 'tgt', scatter_dimension=1, tiled=True)  61.7 us
    psum x1, waiting for transfers between devices, per_device(): col_sums = lax.psum(col_part, 'src')  53.3 us
  transfers between devices with their start and end apart: 6, of which 6 were waited for; matrix products, arithmetic and copies ran while one was open for 5% of the time, Pallas kernels for 0%

commit v1 on v0

--- a/solution.py
+++ b/solution.py
@@ -112,7 +112,9 @@
         start_grads,
         (src_sel_groups, tgt_sel_groups, kernel.reshape(group_count, group_size, BLK, BLK)),
     )
-    tgt_grad = lax.psum(dy_total.reshape(feat_width, tgt_cells), "src")
+    block = dy_total.reshape(feat_width, tgt_cells)
+    pieces = lax.all_gather(block, "src", axis=0, tiled=False)
+    tgt_grad = pieces.sum(axis=0)
     hidden_blocks = src_hidden.reshape(feat_width, src_blocks, BLK)
     grad_share = lax.psum_scatter(dx_total, "tgt", scatter_dimension=1, tiled=True)
     share_blocks = grad_share.shape[1]

time: 1040 us -> 1110 us (1.067)
  waiting for transfers between devices: 371 us -> 437 us
  local copies, waits for them, and re-layouts: 40.3 us -> 25 us
  other arithmetic: 41.4 us -> 55.4 us
    all_gather x0 -> x1, waiting for transfers between devices: none -> 158 us  [per_device(): pieces = lax.all_gather(block, 'src', axis=0, tiled=False)]
    psum x1 -> x0, waiting for transfers between devices: 79.4 us -> none  [per_device(): tgt_grad = lax.psum(dy_total.reshape(feat_width, tgt_cells), 'src')]
    reduce_sum x0 -> x1, other arithmetic: none -> 14 us  [per_device(): tgt_grad = pieces.sum(axis=0)]
    reduce_scatter x1, waiting for transfers between devices: 140 us -> 126 us  [per_device(): lax.psum_scatter(jnp.einsum('kb,bde->kde', owners, outer, precision=highe...]
    unnamed x22 -> x20, local copies, waits for them, and re-layouts: 18.2 us -> 6.76 us
  transfers between devices with their start and end apart: 6 -> 6, of which waited for: 6 -> 6; matrix products, arithmetic and copies ran while one was open for 5% -> 6% of each run, Pallas kernels for 0% -> 0%
where the time goes in v1:
time: 1110 us; the launch traced here: 1100 us
  matrix products  565 us (51%)
  waiting for transfers between devices  437 us (39%)
  other arithmetic  55.4 us (5%)
  local copies, waits for them, and re-layouts  25 us (2%)
  between operations  15.4 us (1%)
    all_gather x1, waiting for transfers between devices, per_device(): pieces = lax.all_gather(block, 'src', axis=0, tiled=False)  158 us
    reduce_scatter x1, waiting for transfers between devices, per_device(): lax.psum_scatter(jnp.einsum('kb,bde->kde', owners, outer, precision=highe...  126 us
    dot_general x2, matrix products, per_device(): row_slots = jnp.einsum('pij,pj->pi', kernel, tgt_picked, precision=highest)  112 us
    dot_general x8, matrix products, gradient_group(): jnp.einsum('gb,dgi->dbi', tgt_sel, dy_term, precision=highest)  89 us
    dot_general x8, matrix products, gradient_group(): jnp.einsum('gb,dgi->dbi', src_sel, dx_term, precision=highest)  88.5 us
    dot_general x2, matrix products, per_device(): col_slots = jnp.einsum('pij,pi->pj', kernel, src_picked, precision=highest)  64.3 us
    reduce_scatter x1, waiting for transfers between devices, per_device(): lax.psum_scatter(dx_total, 'tgt', scatter_dimension=1, tiled=True)  63.3 us
    psum x1, waiting for transfers between devices, per_device(): col_sums = lax.psum(col_part, 'src')  53.3 us
  transfers between devices with their start and end apart: 6, of which 6 were waited for; matrix products, arithmetic and copies ran while one was open for 6% of the time, Pallas kernels for 0%

profile of v1, /device:TPU:0, one launch (start us, length us, event | category | flops | bytes accessed | tf_op | source)
XLA Modules:
  0.0 1099.0 jit_solution(15945523939458369130)
XLA Ops:
  17.6 82.1 %while.23 = (s32[]{:T(128)}, f32[8,64,128,128]{3,2,1,0:T(8,128)}, f32[8,64,128]{2,1,0:T(8,128)S(1)}, f32[128,128]{1,0:T(8,128)S(1)}, f32[8,64,128]{2,1,0:T(8,128...) while((s32[]{:T(128)}, f32[8,64,128,128]{3,2,1,0:T(8,128)}, ...), condition=%wide.region_3.4_spmd, body=%wide.region_2.3_spmd.sunk | while | flops 436207616 | bytes 12945777 | solution.py:64
  21.2 6.6 bitcast_dynamic-update-slice_fusion.2
  31.5 6.6 bitcast_dynamic-update-slice_fusion.2
  41.8 6.6 bitcast_dynamic-update-slice_fusion.2
  52.0 6.6 bitcast_dynamic-update-slice_fusion.2
  62.3 6.6 bitcast_dynamic-update-slice_fusion.2
  72.5 6.6 bitcast_dynamic-update-slice_fusion.2
  82.8 6.6 bitcast_dynamic-update-slice_fusion.2
  93.1 6.6 bitcast_dynamic-update-slice_fusion.2
  100.0 55.7 %fusion.93 = f32[512,1,128]{2,1,0:T(1,128)S(1)} fusion(f32[512,128,128]{2,1,0:T(8,128)} %bitcast.222, f32[512,128,1]{1,2,0:T(1,128)S(1)} %bitcast.238), kind=kOutput, calls=%fused_computation.134 | convolution fusion | flops 100663296 | bytes 34078720 | tf_op jit(solution)/shard_map/pij,pj->pi/dot_general | solution.py:74
  157.5 32.0 %fusion.94 = f32[512,1,128]{2,1,0:T(1,128)S(1)} fusion(f32[512,128,128]{2,1,0:T(8,128)} %bitcast.223, f32[512,128,1]{1,2,0:T(1,128)S(1)} %bitcast.240), kind=kOutput, calls=%fused_computation.135 | convolution fusion | flops 100663296 | bytes 34078720 | tf_op jit(solution)/shard_map/pij,pi->pj/dot_general | solution.py:75
  195.3 32.3 %fusion.96 = f32[512,1,128]{2,1,0:T(1,128)S(1)} fusion(f32[512,128,128]{2,1,0:T(8,128)} %bitcast.224, f32[512,128,1]{1,2,0:T(1,128)S(1)} %bitcast.241), kind=kOutput, calls=%fused_computation.137 | convolution fusion | flops 100663296 | bytes 34078720 | tf_op jit(solution)/shard_map/pij,pi->pj/dot_general | solution.py:75
  228.8 53.3 %all-reduce.9.cloned.1.call-done = (f32[16384]{0:T(1024)}, f32[16384]{0:T(1024)}) async-done(((f32[16384]{0:T(1024)}, f32[16384]{0:T(1024)}), (f32[16384]{0:T(1024)}, f32[16384]{0:T(1024)})) %all-reduce.9.cloned.1.call-update) | async-done | bytes 131088 | tf_op jit(solution)/shard_map/psum | solution.py:79
  283.3 55.9 %fusion.95 = f32[512,1,128]{2,1,0:T(1,128)S(1)} fusion(f32[512,128,128]{2,1,0:T(8,128)} %bitcast.225, f32[512,128,1]{1,2,0:T(1,128)S(1)} %bitcast.239), kind=kOutput, calls=%fused_computation.136 | convolution fusion | flops 100663296 | bytes 34078720 | tf_op jit(solution)/shard_map/pij,pj->pi/dot_general | solution.py:74
  341.2 33.0 %all-reduce.7.cloned.1.call-done = f32[16384]{0:T(1024)} async-done(((f32[16384]{0:T(1024)}), f32[16384]{0:T(1024)}) %all-reduce.7.cloned.1.call-update) | async-done | bytes 65552 | tf_op jit(solution)/shard_map/psum | solution.py:78
  375.8 330.8 %while.24 = (s32[]{:T(128)}, f32[64,128,128]{1,2,0:T(8,128)}, f32[64,128,128]{1,2,0:T(8,128)}, f32[8,64,128]{2,1,0:T(8,128)S(1)}, f32[128,128]{1,0:T(8,128)}, /*...) while((s32[]{:T(128)}, f32[64,128,128]{1,2,0:T(8,128)}, ...), condition=%wide.region_11.12_spmd.clone, body=%wide.region_8.11_spmd.clone.sunk | while | flops 2191507456 | bytes 61508292 | solution.py:110
  378.6 5.4 fusion.189
  390.4 10.6 bitcast_add_fusion.5
  401.0 4.7 fusion.186
  405.7 9.7 bitcast_add_fusion.4
  418.0 5.4 fusion.189
  429.8 11.2 %bitcast_add_fusion.5 = f32[64,128,128]{1,2,0:T(8,128)} fusion(f32[64,128,128]{1,2,0:T(8,128)} %get-tuple-element.364, f32[64,64,128]{2,1,0:T(8,128)} %fusion.189, bf16[64,64,128]{2,1,0:T(8,128)(2,1)} %fusion.183, pred[]{:T(512)S(6)} %compare.16, f32[64,128]{1,0:T(8,128)S(1)} %get-tuple-element.319, f32[8,64,128]{2,1,0:T(8,128)} %get-tuple-element.380, ...), kind=kOutput, calls=%fused_computation.23.clone.1 | convolution fusion | flops 808976384 | bytes 11600385 | tf_op jit(solution)/shard_map/while/body/eval_jaxpr/gb,dgi->dbi/dot_general | solution.py:103
  445.7 11.3 %bitcast_add_fusion.4 = f32[64,128,128]{1,2,0:T(8,128)} fusion(f32[64,128,128]{1,2,0:T(8,128)} %get-tuple-element.363, f32[64,64,128]{2,1,0:T(8,128)S(1)} %fusion.186, bf16[64,64,128]{2,1,0:T(8,128)(2,1)S(1)} %fusion.187, pred[]{:T(512)S(6)} %compare.16, f32[64,128]{1,0:T(8,128)S(1)} %get-tuple-element.318, ...), kind=kOutput, calls=%fused_computation.24.clone.1 | convolution fusion | flops 808976384 | bytes 11599877 | tf_op jit(solution)/shard_map/while/body/eval_jaxpr/gb,dgi->dbi/dot_general | solution.py:102
  459.5 5.4 fusion.189
  471.4 11.2 %bitcast_add_fusion.5 = f32[64,128,128]{1,2,0:T(8,128)} fusion(f32[64,128,128]{1,2,0:T(8,128)} %get-tuple-element.364, f32[64,64,128]{2,1,0:T(8,128)} %fusion.189, bf16[64,64,128]{2,1,0:T(8,128)(2,1)} %fusion.183, pred[]{:T(512)S(6)} %compare.16, f32[64,128]{1,0:T(8,128)S(1)} %get-tuple-element.319, f32[8,64,128]{2,1,0:T(8,128)} %get-tuple-element.380, ...), kind=kOutput, calls=%fused_computation.23.clone.1 | convolution fusion | flops 808976384 | bytes 11600385 | tf_op jit(solution)/shard_map/while/body/eval_jaxpr/gb,dgi->dbi/dot_general | solution.py:103
  487.3 11.3 %bitcast_add_fusion.4 = f32[64,128,128]{1,2,0:T(8,128)} fusion(f32[64,128,128]{1,2,0:T(8,128)} %get-tuple-element.363, f32[64,64,128]{2,1,0:T(8,128)S(1)} %fusion.186, bf16[64,64,128]{2,1,0:T(8,128)(2,1)S(1)} %fusion.187, pred[]{:T(512)S(6)} %compare.16, f32[64,128]{1,0:T(8,128)S(1)} %get-tuple-element.318, ...), kind=kOutput, calls=%fused_computation.24.clone.1 | convolution fusion | flops 808976384 | bytes 11599877 | tf_op jit(solution)/shard_map/while/body/eval_jaxpr/gb,dgi->dbi/dot_general | solution.py:102
  501.1 5.4 fusion.189
  512.9 11.2 %bitcast_add_fusion.5 = f32[64,128,128]{1,2,0:T(8,128)} fusion(f32[64,128,128]{1,2,0:T(8,128)} %get-tuple-element.364, f32[64,64,128]{2,1,0:T(8,128)} %fusion.189, bf16[64,64,128]{2,1,0:T(8,128)(2,1)} %fusion.183, pred[]{:T(512)S(6)} %compare.16, f32[64,128]{1,0:T(8,128)S(1)} %get-tuple-element.319, f32[8,64,128]{2,1,0:T(8,128)} %get-tuple-element.380, ...), kind=kOutput, calls=%fused_computation.23.clone.1 | convolution fusion | flops 808976384 | bytes 11600385 | tf_op jit(solution)/shard_map/while/body/eval_jaxpr/gb,dgi->dbi/dot_general | solution.py:103
  528.9 11.3 %bitcast_add_fusion.4 = f32[64,128,128]{1,2,0:T(8,128)} fusion(f32[64,128,128]{1,2,0:T(8,128)} %get-tuple-element.363, f32[64,64,128]{2,1,0:T(8,128)S(1)} %fusion.186, bf16[64,64,128]{2,1,0:T(8,128)(2,1)S(1)} %fusion.187, pred[]{:T(512)S(6)} %compare.16, f32[64,128]{1,0:T(8,128)S(1)} %get-tuple-element.318, ...), kind=kOutput, calls=%fused_computation.24.clone.1 | convolution fusion | flops 808976384 | bytes 11599877 | tf_op jit(solution)/shard_map/while/body/eval_jaxpr/gb,dgi->dbi/dot_general | solution.py:102
  542.6 5.4 fusion.189
  554.5 11.2 %bitcast_add_fusion.5 = f32[64,128,128]{1,2,0:T(8,128)} fusion(f32[64,128,128]{1,2,0:T(8,128)} %get-tuple-element.364, f32[64,64,128]{2,1,0:T(8,128)} %fusion.189, bf16[64,64,128]{2,1,0:T(8,128)(2,1)} %fusion.183, pred[]{:T(512)S(6)} %compare.16, f32[64,128]{1,0:T(8,128)S(1)} %get-tuple-element.319, f32[8,64,128]{2,1,0:T(8,128)} %get-tuple-element.380, ...), kind=kOutput, calls=%fused_computation.23.clone.1 | convolution fusion | flops 808976384 | bytes 11600385 | tf_op jit(solution)/shard_map/while/body/eval_jaxpr/gb,dgi->dbi/dot_general | solution.py:103
  570.4 11.3 %bitcast_add_fusion.4 = f32[64,128,128]{1,2,0:T(8,128)} fusion(f32[64,128,128]{1,2,0:T(8,128)} %get-tuple-element.363, f32[64,64,128]{2,1,0:T(8,128)S(1)} %fusion.186, bf16[64,64,128]{2,1,0:T(8,128)(2,1)S(1)} %fusion.187, pred[]{:T(512)S(6)} %compare.16, f32[64,128]{1,0:T(8,128)S(1)} %get-tuple-element.318, ...), kind=kOutput, calls=%fused_computation.24.clone.1 | convolution fusion | flops 808976384 | bytes 11599877 | tf_op jit(solution)/shard_map/while/body/eval_jaxpr/gb,dgi->dbi/dot_general | solution.py:102
  584.2 5.4 fusion.189
  596.1 11.2 %bitcast_add_fusion.5 = f32[64,128,128]{1,2,0:T(8,128)} fusion(f32[64,128,128]{1,2,0:T(8,128)} %get-tuple-element.364, f32[64,64,128]{2,1,0:T(8,128)} %fusion.189, bf16[64,64,128]{2,1,0:T(8,128)(2,1)} %fusion.183, pred[]{:T(512)S(6)} %compare.16, f32[64,128]{1,0:T(8,128)S(1)} %get-tuple-element.319, f32[8,64,128]{2,1,0:T(8,128)} %get-tuple-element.380, ...), kind=kOutput, calls=%fused_computation.23.clone.1 | convolution fusion | flops 808976384 | bytes 11600385 | tf_op jit(solution)/shard_map/while/body/eval_jaxpr/gb,dgi->dbi/dot_general | solution.py:103
  612.0 11.3 %bitcast_add_fusion.4 = f32[64,128,128]{1,2,0:T(8,128)} fusion(f32[64,128,128]{1,2,0:T(8,128)} %get-tuple-element.363, f32[64,64,128]{2,1,0:T(8,128)S(1)} %fusion.186, bf16[64,64,128]{2,1,0:T(8,128)(2,1)S(1)} %fusion.187, pred[]{:T(512)S(6)} %compare.16, f32[64,128]{1,0:T(8,128)S(1)} %get-tuple-element.318, ...), kind=kOutput, calls=%fused_computation.24.clone.1 | convolution fusion | flops 808976384 | bytes 11599877 | tf_op jit(solution)/shard_map/while/body/eval_jaxpr/gb,dgi->dbi/dot_general | solution.py:102
  625.8 5.4 fusion.189
  637.6 11.2 %bitcast_add_fusion.5 = f32[64,128,128]{1,2,0:T(8,128)} fusion(f32[64,128,128]{1,2,0:T(8,128)} %get-tuple-element.364, f32[64,64,128]{2,1,0:T(8,128)} %fusion.189, bf16[64,64,128]{2,1,0:T(8,128)(2,1)} %fusion.183, pred[]{:T(512)S(6)} %compare.16, f32[64,128]{1,0:T(8,128)S(1)} %get-tuple-element.319, f32[8,64,128]{2,1,0:T(8,128)} %get-tuple-element.380, ...), kind=kOutput, calls=%fused_computation.23.clone.1 | convolution fusion | flops 808976384 | bytes 11600385 | tf_op jit(solution)/shard_map/while/body/eval_jaxpr/gb,dgi->dbi/dot_general | solution.py:103
  653.5 11.3 %bitcast_add_fusion.4 = f32[64,128,128]{1,2,0:T(8,128)} fusion(f32[64,128,128]{1,2,0:T(8,128)} %get-tuple-element.363, f32[64,64,128]{2,1,0:T(8,128)S(1)} %fusion.186, bf16[64,64,128]{2,1,0:T(8,128)(2,1)S(1)} %fusion.187, pred[]{:T(512)S(6)} %compare.16, f32[64,128]{1,0:T(8,128)S(1)} %get-tuple-element.318, ...), kind=kOutput, calls=%fused_computation.24.clone.1 | convolution fusion | flops 808976384 | bytes 11599877 | tf_op jit(solution)/shard_map/while/body/eval_jaxpr/gb,dgi->dbi/dot_general | solution.py:102
  667.3 5.4 fusion.189
  679.2 11.2 %bitcast_add_fusion.5 = f32[64,128,128]{1,2,0:T(8,128)} fusion(f32[64,128,128]{1,2,0:T(8,128)} %get-tuple-element.364, f32[64,64,128]{2,1,0:T(8,128)} %fusion.189, bf16[64,64,128]{2,1,0:T(8,128)(2,1)} %fusion.183, pred[]{:T(512)S(6)} %compare.16, f32[64,128]{1,0:T(8,128)S(1)} %get-tuple-element.319, f32[8,64,128]{2,1,0:T(8,128)} %get-tuple-element.380, ...), kind=kOutput, calls=%fused_computation.23.clone.1 | convolution fusion | flops 808976384 | bytes 11600385 | tf_op jit(solution)/shard_map/while/body/eval_jaxpr/gb,dgi->dbi/dot_general | solution.py:103
  695.1 11.3 %bitcast_add_fusion.4 = f32[64,128,128]{1,2,0:T(8,128)} fusion(f32[64,128,128]{1,2,0:T(8,128)} %get-tuple-element.363, f32[64,64,128]{2,1,0:T(8,128)S(1)} %fusion.186, bf16[64,64,128]{2,1,0:T(8,128)(2,1)S(1)} %fusion.187, pred[]{:T(512)S(6)} %compare.16, f32[64,128]{1,0:T(8,128)S(1)} %get-tuple-element.318, ...), kind=kOutput, calls=%fused_computation.24.clone.1 | convolution fusion | flops 808976384 | bytes 11599877 | tf_op jit(solution)/shard_map/while/body/eval_jaxpr/gb,dgi->dbi/dot_general | solution.py:102
  706.6 5.4 copy.33
  712.1 5.6 copy.31
  717.7 5.3 all_gather_reshape.3
  725.3 63.3 %reduce-scatter.3.cloned.1.call-done = f32[64,32,128]{2,0,1:T(8,128)} async-done(((f32[64,128,128]{2,0,1:T(8,128)}), f32[64,32,128]{2,0,1:T(8,128)}) %reduce-scatter.3.cloned.1.call-update) | async-done | bytes 1048592 | tf_op jit(solution)/shard_map/reduce_scatter | solution.py:119
  793.8 157.8 %all-gather.2.cloned.1.call-done = f32[8,64,16384]{2,1,0:T(8,128)} async-done(((f32[1,64,16384]{2,1,0:T(8,128)}), f32[8,64,16384]{2,1,0:T(8,128)}) %all-gather.2.cloned.1.call-update) | async-done | bytes 33554448 | tf_op jit(solution)/shard_map/all_gather | solution.py:116
  951.6 14.0 %reduce_sum.53 = f32[64,16384]{1,0:T(8,128)} reduce(f32[8,64,16384]{2,1,0:T(8,128)} %all-gather.2.cloned.1.call-done, f32[]{:T(128)} %constant.71.clone.1), dimensions={0}, to_apply=%region_12.13 | reduce | flops 7340032 | bytes 37748740 | tf_op jit(solution)/shard_map/reduce_sum | solution.py:117
  965.6 126.1 %reduce-scatter.5.cloned.1.call-done = f32[1,64,64]{2,1,0:T(8,128)} async-done(((f32[32,64,64]{2,1,0:T(8,128)}), f32[1,64,64]{2,1,0:T(8,128)}) %reduce-scatter.5.cloned.1.call-update) | async-done | bytes 16400 | tf_op jit(solution)/shard_map/reduce_scatter | solution.py:130
  (178 shorter events, 164.2 us)
Async XLA Ops:
  7.2 186.9 %all-reduce.5.cloned.1.call-start = ((), (), s32[]{:S(2)}) async-start(), calls=%async_computation.2 | async-start | bytes 131072 | tf_op jit(solution)/shard_map/psum | solution.py:78
  9.2 4.4 copy-start.2
  17.6 82.1 %copy-start.8 = (s32[1,1,512]{2,1,0:T(1,128)S(1)}, s32[1,1,512]{2,1,0:T(1,128)}, u32[]{:S(2)}) copy-start(s32[1,1,512]{2,1,0:T(1,128)} %param.17) | copy-start | bytes 6148
  156.9 125.2 %all-reduce.9.cloned.1.call-start = ((), (), s32[]{:S(2)}) async-start(), calls=%async_computation.7 | async-start | bytes 262144 | tf_op jit(solution)/shard_map/psum | solution.py:79
  157.5 36.6 %copy-start.4 = (f32[16384]{0:T(1024)S(1)}, f32[16384]{0:T(1024)}, u32[]{:S(2)}) copy-start(f32[16384]{0:T(1024)} %param.15) | copy-start | bytes 196612
  195.2 86.9 %copy-start.3 = (f32[16384]{0:T(1024)S(1)}, f32[16384]{0:T(1024)}, u32[]{:S(2)}) copy-start(f32[16384]{0:T(1024)} %param.16) | copy-start | bytes 196612
  228.8 145.4 %all-reduce.7.cloned.1.call-start = ((), (), s32[]{:S(2)}) async-start(), calls=%async_computation.3 | async-start | bytes 131072 | tf_op jit(solution)/shard_map/psum | solution.py:78
  283.3 57.1 %copy-start.6 = (f32[16384]{0:T(1024)S(1)}, f32[16384]{0:T(1024)}, u32[]{:S(2)}) copy-start(f32[16384]{0:T(1024)} %get-tuple-element.188) | copy-start | bytes 196612
  283.3 57.1 %copy-start.7 = (f32[16384]{0:T(1024)S(1)}, f32[16384]{0:T(1024)}, u32[]{:S(2)}) copy-start(f32[16384]{0:T(1024)} %get-tuple-element.189) | copy-start | bytes 196612
  283.3 90.9 %copy-start.5 = (f32[16384]{0:T(1024)S(1)}, f32[16384]{0:T(1024)}, u32[]{:S(2)}) copy-start(f32[16384]{0:T(1024)} %all-reduce.5.cloned.1.call-done) | copy-start | bytes 196612
  340.4 448.3 %reduce-scatter.3.cloned.1.call-start = ((), (), s32[]{:S(2)}) async-start(), calls=%async_computation.5 | async-start | bytes 5242880 | tf_op jit(solution)/shard_map/reduce_scatter | solution.py:119
  378.5 9.7 copy-start
  390.4 10.6 copy-start.1
  417.9 9.7 copy-start
  429.8 11.2 %copy-start.1 = (bf16[64,64,128]{2,1,0:T(8,128)(2,1)S(1)}, bf16[64,64,128]{2,1,0:T(8,128)(2,1)}, u32[]{:S(2)}) copy-start(bf16[64,64,128]{2,1,0:T(8,128)(2,1)} %fusion.183) | copy-start | bytes 3145732 | tf_op jit(solution)/shard_map/while
  459.5 9.7 copy-start
  471.4 11.2 %copy-start.1 = (bf16[64,64,128]{2,1,0:T(8,128)(2,1)S(1)}, bf16[64,64,128]{2,1,0:T(8,128)(2,1)}, u32[]{:S(2)}) copy-start(bf16[64,64,128]{2,1,0:T(8,128)(2,1)} %fusion.183) | copy-start | bytes 3145732 | tf_op jit(solution)/shard_map/while
  501.1 9.7 copy-start
  512.9 11.2 %copy-start.1 = (bf16[64,64,128]{2,1,0:T(8,128)(2,1)S(1)}, bf16[64,64,128]{2,1,0:T(8,128)(2,1)}, u32[]{:S(2)}) copy-start(bf16[64,64,128]{2,1,0:T(8,128)(2,1)} %fusion.183) | copy-start | bytes 3145732 | tf_op jit(solution)/shard_map/while
  542.6 9.7 copy-start
  554.5 11.2 %copy-start.1 = (bf16[64,64,128]{2,1,0:T(8,128)(2,1)S(1)}, bf16[64,64,128]{2,1,0:T(8,128)(2,1)}, u32[]{:S(2)}) copy-start(bf16[64,64,128]{2,1,0:T(8,128)(2,1)} %fusion.183) | copy-start | bytes 3145732 | tf_op jit(solution)/shard_map/while
  584.2 9.7 copy-start
  596.1 11.2 %copy-start.1 = (bf16[64,64,128]{2,1,0:T(8,128)(2,1)S(1)}, bf16[64,64,128]{2,1,0:T(8,128)(2,1)}, u32[]{:S(2)}) copy-start(bf16[64,64,128]{2,1,0:T(8,128)(2,1)} %fusion.183) | copy-start | bytes 3145732 | tf_op jit(solution)/shard_map/while
  625.8 9.7 copy-start
  637.6 11.2 %copy-start.1 = (bf16[64,64,128]{2,1,0:T(8,128)(2,1)S(1)}, bf16[64,64,128]{2,1,0:T(8,128)(2,1)}, u32[]{:S(2)}) copy-start(bf16[64,64,128]{2,1,0:T(8,128)(2,1)} %fusion.183) | copy-start | bytes 3145732 | tf_op jit(solution)/shard_map/while
  667.3 9.7 copy-start
  679.2 11.2 %copy-start.1 = (bf16[64,64,128]{2,1,0:T(8,128)(2,1)S(1)}, bf16[64,64,128]{2,1,0:T(8,128)(2,1)}, u32[]{:S(2)}) copy-start(bf16[64,64,128]{2,1,0:T(8,128)(2,1)} %fusion.183) | copy-start | bytes 3145732 | tf_op jit(solution)/shard_map/while
  712.0 239.6 %all-gather.2.cloned.1.call-start = ((), (), s32[]{:S(2)}) async-start(), calls=%async_computation.4 | async-start | bytes 37748736 | tf_op jit(solution)/shard_map/all_gather | solution.py:116
  723.0 2.3 copy-start.9
  723.0 368.7 %reduce-scatter.5.cloned.1.call-start = ((), (), s32[]{:S(2)}) async-start(), calls=%async_computation.6 | async-start | bytes 1081344 | tf_op jit(solution)/shard_map/reduce_scatter | solution.py:130
Sparse Core Ops, SparseCore 0:
  157.0 37.0 all-reduce.4
  228.9 53.2 all-reduce.8
  340.5 33.6 all-reduce.6
  712.1 76.4 reduce-scatter.2
  790.4 161.1 all-gather.1
  954.3 137.3 reduce-scatter.4
